TPU v7x, 128 devices: a whole 4x4x4 slice. The times are simulated.
128 devices in a mesh: tok: 32 (over y, x, core), kv: 4 (over z).
Axes of the slice: x: 4, y: 4, z: 4, core: 2. Of those that a mesh axis runs over, the one named last changes fastest.
Arguments:
- queries: bfloat16 [8192, 8192], P('tok', 'kv'), may hold values from -12 to 12
- key_states: bfloat16 [8192, 1024], P('tok', 'kv'), may hold values from -12 to 12
- value_states: bfloat16 [8192, 1024], P('tok', 'kv'), may hold values from -6 to 6
- doc_lengths: int32 [16], replicated, may hold values from 1 to 4096, 8192 in all
- block_plan: int32 [32, 32], replicated, may hold values from 0 to 31, each once within a row
Outputs:
- attention_out: bfloat16 [8192, 8192], P(('tok', 'kv'))
- served_lse: float32 [64, 8192], P('kv', 'tok')
Inputs may be any that keep to these rules, and one draw needn't show every extreme that they name: `doc_lengths`: positive lengths that sum to 8192; the largest is exactly 4096. Every row of block_plan is a permutation of 0 to 31.
All inputs are finite; a program needn't handle non-finite values.
Results may differ from a plain program's by a relative error of at most 0.012.
The roundings to bfloat16 on the way count: a program that leaves them out, or rounds other values in their place, can miss the bound.
Values may be sent and summed in bfloat16 or wider, within the bound.
A program may use at most 64 MiB of HBM per device.

v0:
```python
from functools import partial
import math
import jax
import jax.numpy as jnp
from jax import lax
from jax.sharding import PartitionSpec as P

HEAD_DIM = 128
THETA = 500000.0
NEG = -1e30


def doc_layout(doc_lengths, token_index):
    doc_ends = jnp.cumsum(doc_lengths)
    passed = token_index[:, None] >= doc_ends[None, :]
    doc_ids = jnp.sum(passed.astype(jnp.int32), axis=1)
    starts = jnp.sum(jnp.where(passed, doc_lengths[None, :], 0), axis=1)
    return (doc_ids, token_index - starts)


def rotate(inputs, positions, heads):
    half_dim = HEAD_DIM // 2
    inv_freq = jnp.power(
        jnp.float32(THETA), -(jnp.arange(half_dim, dtype=jnp.float32) * 2.0 / HEAD_DIM)
    )
    angles = positions.astype(jnp.float32)[:, None] * inv_freq[None, :]
    cosine = jnp.cos(angles)[:, None, :]
    sine_val = jnp.sin(angles)[:, None, :]
    shaped = inputs.astype(jnp.float32).reshape(inputs.shape[0], heads, HEAD_DIM)
    leading = shaped[..., :half_dim]
    trailing = shaped[..., half_dim:]
    turned = jnp.concatenate(
        [leading * cosine - trailing * sine_val, trailing * cosine + leading * sine_val], axis=-1
    )
    return turned.reshape(inputs.shape[0], heads * HEAD_DIM).astype(jnp.bfloat16)


def attend_block(
    carry_state, query_rows, query_index, query_docs, key_rows, value_rows, key_index, key_docs
):
    row_max, row_sum, weighted = carry_state
    score_scale = 1.0 / math.sqrt(HEAD_DIM)
    scores = (
        jnp.einsum("rgqd,ngd->gqrn", query_rows, key_rows, preferred_element_type=jnp.float32)
        * score_scale
    )
    allowed = (
        (query_docs[:, None] == key_docs[None, :])
        & (key_index[None, :] <= query_index[:, None])
        & (key_index[None, :] >= 0)
    )
    scores = jnp.where(allowed, scores, NEG)
    new_max = jnp.maximum(row_max, jnp.max(scores, axis=-1))
    weights = jnp.where(allowed, jnp.exp(scores - new_max[..., None]), 0.0)
    factor = jnp.exp(row_max - new_max)
    row_sum = row_sum * factor + jnp.sum(weights, axis=-1)
    probs = weights.astype(jnp.bfloat16)
    weighted = weighted * factor[..., None] + jnp.einsum(
        "gqrn,ngd->gqrd", probs, value_rows, preferred_element_type=jnp.float32
    )
    return (new_max, row_sum, weighted)


def fold_keys(
    carry_state, piece, start, query_rows=None, query_index=None, query_docs=None, doc_lengths=None
):
    key_piece, value_piece = piece
    count = key_piece.shape[0]
    stride = math.gcd(count, 512)
    kv_local = key_piece.shape[1] // HEAD_DIM

    def inner(counter, running):
        offset = counter * stride
        key_rows = lax.dynamic_slice_in_dim(key_piece, offset, stride, 0).reshape(
            stride, kv_local, HEAD_DIM
        )
        value_rows = lax.dynamic_slice_in_dim(value_piece, offset, stride, 0).reshape(
            stride, kv_local, HEAD_DIM
        )
        key_index = offset + jnp.arange(stride, dtype=jnp.int32)
        key_docs, unused_pos = doc_layout(doc_lengths, key_index)
        return attend_block(
            running, query_rows, query_index, query_docs, key_rows, value_rows, key_index, key_docs
        )

    return lax.fori_loop(0, count // stride, inner, carry_state)


def finish(carry_state, rows, q_local):
    row_max, row_sum, weighted = carry_state
    mixed = weighted / row_sum[..., None]
    result = (
        jnp.transpose(mixed, (2, 0, 1, 3)).reshape(rows, q_local * HEAD_DIM).astype(jnp.bfloat16)
    )
    log_norm = (row_max + jnp.log(row_sum)).reshape(q_local, rows)
    return (result, log_norm)


def body(queries, key_states, value_states, doc_lengths, block_plan):
    shards = lax.axis_size("tok")
    shard_index = lax.axis_index("tok")
    tok_dev = queries.shape[0]
    block_rows = tok_dev // shards
    kv_local = key_states.shape[1] // HEAD_DIM
    q_local = queries.shape[1] // HEAD_DIM
    per_group = q_local // kv_local
    token_index = shard_index * tok_dev + jnp.arange(tok_dev, dtype=jnp.int32)
    doc_ids, positions = doc_layout(doc_lengths, token_index)
    q_rot = rotate(queries, positions, q_local)
    k_rot = rotate(key_states, positions, kv_local)
    my_blocks = lax.dynamic_index_in_dim(block_plan, shard_index, 0, keepdims=False)
    initial = (
        jnp.full((kv_local, per_group, tok_dev), NEG, jnp.float32),
        jnp.zeros((kv_local, per_group, tok_dev), jnp.float32),
        jnp.zeros((kv_local, per_group, tok_dev, HEAD_DIM), jnp.float32),
    )
    plan_column = lax.dynamic_index_in_dim(block_plan, shard_index, 1, keepdims=False)
    outgoing = jnp.take(q_rot.reshape(shards, block_rows, q_local * HEAD_DIM), my_blocks, axis=0)
    incoming = lax.all_to_all(outgoing, "tok", split_axis=0, concat_axis=0, tiled=True)
    served_index = (
        jnp.arange(shards, dtype=jnp.int32)[:, None] * tok_dev
        + plan_column[:, None] * block_rows
        + jnp.arange(block_rows, dtype=jnp.int32)[None, :]
    ).reshape(tok_dev)
    served_docs, unused_pos = doc_layout(doc_lengths, served_index)
    served_rows = incoming.reshape(tok_dev, kv_local, per_group, HEAD_DIM)
    folder = partial(
        fold_keys,
        query_rows=served_rows,
        query_index=served_index,
        query_docs=served_docs,
        doc_lengths=doc_lengths,
    )
    final_state = folder(
        initial,
        (
            lax.all_gather(k_rot, "tok", axis=0, tiled=True),
            lax.all_gather(value_states, "tok", axis=0, tiled=True),
        ),
        jnp.int32(0),
    )
    result, served_lse = finish(final_state, tok_dev, q_local)
    returned = lax.all_to_all(
        result.reshape(shards, block_rows, q_local * HEAD_DIM),
        "tok",
        split_axis=0,
        concat_axis=0,
        tiled=True,
    )
    ordered = (
        jnp.zeros_like(returned).at[my_blocks].set(returned).reshape(tok_dev, q_local * HEAD_DIM)
    )
    attention_out = lax.all_to_all(ordered, "kv", split_axis=0, concat_axis=1, tiled=True)
    return (attention_out, served_lse)


def solution(mesh):
    return jax.shard_map(
        body,
        mesh=mesh,
        in_specs=(P("tok", "kv"), P("tok", "kv"), P("tok", "kv"), P(), P()),
        out_specs=(P(("tok", "kv"), None), P("kv", "tok")),
        check_vma=False,
    )
```

profile of v0, /device:TPU:0, one launch (start us, length us, event | category | flops | bytes accessed | tf_op | source)
XLA Modules:
  0.0 487.8 jit_solution(9570828459599723917)
XLA Ops:
  22.5 7.6 %all-to-all-start = ((bf16[32,8,2048]{2,1,0:T(8,128)(2,1)}), bf16[32,8,2048]{2,1,0:T(8,128)(2,1)S(1)}, u32[]{:S(2)}, u32[]{:S(2)}) async-start(bf16[32,8,2048]{2,1,0:T(8,128)(2,1)} %broadcast_select_fusion), calls=%async_computation | async-start | bytes 2097152 | tf_op jit(solution)/shard_map/all_to_all | solution.py:119
  30.1 18.3 %all-to-all-done = bf16[32,8,2048]{2,1,0:T(8,128)(2,1)S(1)} async-done(((bf16[32,8,2048]{2,1,0:T(8,128)(2,1)}), bf16[32,8,2048]{2,1,0:T(8,128)(2,1)S(1)}, u32[]{:S(2)}, u32[]{:S(2)}) %all-to-all-start) | async-done | bytes 1048608 | tf_op jit(solution)/shard_map/all_to_all | solution.py:119
  48.9 24.8 %all-gather.3.cloned.1.call-done = bf16[8192,256]{0,1:T(8,128)(2,1)} async-done(((bf16[256,256]{0,1:T(8,128)(2,1)}), bf16[8192,256]{0,1:T(8,128)(2,1)}) %all-gather.3.cloned.1.call-update) | async-done | bytes 4194320 | tf_op jit(solution)/shard_map/all_gather | solution.py:137
  73.7 50.9 %all-gather.5.cloned.1.call-done = bf16[8192,256]{0,1:T(8,128)(2,1)} async-done(((bf16[256,256]{0,1:T(8,128)(2,1)}), bf16[8192,256]{0,1:T(8,128)(2,1)}) %all-gather.5.cloned.1.call-update) | async-done | bytes 4194320 | tf_op jit(solution)/shard_map/all_gather | solution.py:138
  124.6 304.6 %while.20 = (s32[]{:T(128)}, f32[2,8,256]{2,1,0:T(8,128)S(1)}, f32[2,8,256]{2,1,0:T(8,128)}, f32[2,8,256,128]{3,2,1,0:T(8,128)S(1)}, s32[256]{0:T(256)}, /*index...) while((s32[]{:T(128)}, f32[2,8,256]{2,1,0:T(8,128)S(1)}, ...), condition=%wide.region_7.8_spmd.clone, body=%wide.region_3.7_spmd.clone.sunk | while | flops 1103148288 | bytes 66470364 | solution.py:86
  128.2 5.3 %fusion.32 = (f32[2,8,256]{2,1,0:T(8,128)}, f32[2,512,256,8]{2,1,3,0:T(8,128)}) fusion(pred[256,512]{0,1:T(8,128)(4,1)S(1)} %and_and_fusion.2, bf16[512,2,128,1]{0,2,3,1:T(8,128)(2,1)S(1)} %bitcast.72, bf16[256,2,8,128]{3,0,2,1:T(8,128)(2,1)S(1)} %get-tuple-element.448), kind=kOutput, calls=%fused_computation.5.clone.1 | convolution fusion | flops 543158272 | bytes 9846784 | tf_op jit(solution)/shard_map/while/body/eval_jaxpr/rgqd,ngd->gqrn/dot_general | solution.py:44
  134.3 4.6 fusion.33
  147.3 5.3 %fusion.32 = (f32[2,8,256]{2,1,0:T(8,128)}, f32[2,512,256,8]{2,1,3,0:T(8,128)}) fusion(pred[256,512]{0,1:T(8,128)(4,1)S(1)} %and_and_fusion.2, bf16[512,2,128,1]{0,2,3,1:T(8,128)(2,1)S(1)} %bitcast.72, bf16[256,2,8,128]{3,0,2,1:T(8,128)(2,1)S(1)} %get-tuple-element.448), kind=kOutput, calls=%fused_computation.5.clone.1 | convolution fusion | flops 543158272 | bytes 9846784 | tf_op jit(solution)/shard_map/while/body/eval_jaxpr/rgqd,ngd->gqrn/dot_general | solution.py:44
  153.3 4.6 fusion.33
  166.3 5.3 %fusion.32 = (f32[2,8,256]{2,1,0:T(8,128)}, f32[2,512,256,8]{2,1,3,0:T(8,128)}) fusion(pred[256,512]{0,1:T(8,128)(4,1)S(1)} %and_and_fusion.2, bf16[512,2,128,1]{0,2,3,1:T(8,128)(2,1)S(1)} %bitcast.72, bf16[256,2,8,128]{3,0,2,1:T(8,128)(2,1)S(1)} %get-tuple-element.448), kind=kOutput, calls=%fused_computation.5.clone.1 | convolution fusion | flops 543158272 | bytes 9846784 | tf_op jit(solution)/shard_map/while/body/eval_jaxpr/rgqd,ngd->gqrn/dot_general | solution.py:44
  172.4 4.6 fusion.33
  185.3 5.3 %fusion.32 = (f32[2,8,256]{2,1,0:T(8,128)}, f32[2,512,256,8]{2,1,3,0:T(8,128)}) fusion(pred[256,512]{0,1:T(8,128)(4,1)S(1)} %and_and_fusion.2, bf16[512,2,128,1]{0,2,3,1:T(8,128)(2,1)S(1)} %bitcast.72, bf16[256,2,8,128]{3,0,2,1:T(8,128)(2,1)S(1)} %get-tuple-element.448), kind=kOutput, calls=%fused_computation.5.clone.1 | convolution fusion | flops 543158272 | bytes 9846784 | tf_op jit(solution)/shard_map/while/body/eval_jaxpr/rgqd,ngd->gqrn/dot_general | solution.py:44
  191.4 4.6 fusion.33
  204.4 5.3 %fusion.32 = (f32[2,8,256]{2,1,0:T(8,128)}, f32[2,512,256,8]{2,1,3,0:T(8,128)}) fusion(pred[256,512]{0,1:T(8,128)(4,1)S(1)} %and_and_fusion.2, bf16[512,2,128,1]{0,2,3,1:T(8,128)(2,1)S(1)} %bitcast.72, bf16[256,2,8,128]{3,0,2,1:T(8,128)(2,1)S(1)} %get-tuple-element.448), kind=kOutput, calls=%fused_computation.5.clone.1 | convolution fusion | flops 543158272 | bytes 9846784 | tf_op jit(solution)/shard_map/while/body/eval_jaxpr/rgqd,ngd->gqrn/dot_general | solution.py:44
  210.4 4.6 fusion.33
  223.4 5.3 %fusion.32 = (f32[2,8,256]{2,1,0:T(8,128)}, f32[2,512,256,8]{2,1,3,0:T(8,128)}) fusion(pred[256,512]{0,1:T(8,128)(4,1)S(1)} %and_and_fusion.2, bf16[512,2,128,1]{0,2,3,1:T(8,128)(2,1)S(1)} %bitcast.72, bf16[256,2,8,128]{3,0,2,1:T(8,128)(2,1)S(1)} %get-tuple-element.448), kind=kOutput, calls=%fused_computation.5.clone.1 | convolution fusion | flops 543158272 | bytes 9846784 | tf_op jit(solution)/shard_map/while/body/eval_jaxpr/rgqd,ngd->gqrn/dot_general | solution.py:44
  229.5 4.6 fusion.33
  242.5 5.3 %fusion.32 = (f32[2,8,256]{2,1,0:T(8,128)}, f32[2,512,256,8]{2,1,3,0:T(8,128)}) fusion(pred[256,512]{0,1:T(8,128)(4,1)S(1)} %and_and_fusion.2, bf16[512,2,128,1]{0,2,3,1:T(8,128)(2,1)S(1)} %bitcast.72, bf16[256,2,8,128]{3,0,2,1:T(8,128)(2,1)S(1)} %get-tuple-element.448), kind=kOutput, calls=%fused_computation.5.clone.1 | convolution fusion | flops 543158272 | bytes 9846784 | tf_op jit(solution)/shard_map/while/body/eval_jaxpr/rgqd,ngd->gqrn/dot_general | solution.py:44
  248.5 4.6 fusion.33
  261.5 5.3 %fusion.32 = (f32[2,8,256]{2,1,0:T(8,128)}, f32[2,512,256,8]{2,1,3,0:T(8,128)}) fusion(pred[256,512]{0,1:T(8,128)(4,1)S(1)} %and_and_fusion.2, bf16[512,2,128,1]{0,2,3,1:T(8,128)(2,1)S(1)} %bitcast.72, bf16[256,2,8,128]{3,0,2,1:T(8,128)(2,1)S(1)} %get-tuple-element.448), kind=kOutput, calls=%fused_computation.5.clone.1 | convolution fusion | flops 543158272 | bytes 9846784 | tf_op jit(solution)/shard_map/while/body/eval_jaxpr/rgqd,ngd->gqrn/dot_general | solution.py:44
  267.6 4.6 fusion.33
  280.5 5.3 %fusion.32 = (f32[2,8,256]{2,1,0:T(8,128)}, f32[2,512,256,8]{2,1,3,0:T(8,128)}) fusion(pred[256,512]{0,1:T(8,128)(4,1)S(1)} %and_and_fusion.2, bf16[512,2,128,1]{0,2,3,1:T(8,128)(2,1)S(1)} %bitcast.72, bf16[256,2,8,128]{3,0,2,1:T(8,128)(2,1)S(1)} %get-tuple-element.448), kind=kOutput, calls=%fused_computation.5.clone.1 | convolution fusion | flops 543158272 | bytes 9846784 | tf_op jit(solution)/shard_map/while/body/eval_jaxpr/rgqd,ngd->gqrn/dot_general | solution.py:44
  286.6 4.6 fusion.33
  299.6 5.3 %fusion.32 = (f32[2,8,256]{2,1,0:T(8,128)}, f32[2,512,256,8]{2,1,3,0:T(8,128)}) fusion(pred[256,512]{0,1:T(8,128)(4,1)S(1)} %and_and_fusion.2, bf16[512,2,128,1]{0,2,3,1:T(8,128)(2,1)S(1)} %bitcast.72, bf16[256,2,8,128]{3,0,2,1:T(8,128)(2,1)S(1)} %get-tuple-element.448), kind=kOutput, calls=%fused_computation.5.clone.1 | convolution fusion | flops 543158272 | bytes 9846784 | tf_op jit(solution)/shard_map/while/body/eval_jaxpr/rgqd,ngd->gqrn/dot_general | solution.py:44
  318.6 5.3 %fusion.32 = (f32[2,8,256]{2,1,0:T(8,128)}, f32[2,512,256,8]{2,1,3,0:T(8,128)}) fusion(pred[256,512]{0,1:T(8,128)(4,1)S(1)} %and_and_fusion.2, bf16[512,2,128,1]{0,2,3,1:T(8,128)(2,1)S(1)} %bitcast.72, bf16[256,2,8,128]{3,0,2,1:T(8,128)(2,1)S(1)} %get-tuple-element.448), kind=kOutput, calls=%fused_computation.5.clone.1 | convolution fusion | flops 543158272 | bytes 9846784 | tf_op jit(solution)/shard_map/while/body/eval_jaxpr/rgqd,ngd->gqrn/dot_general | solution.py:44
  337.7 5.3 %fusion.32 = (f32[2,8,256]{2,1,0:T(8,128)}, f32[2,512,256,8]{2,1,3,0:T(8,128)}) fusion(pred[256,512]{0,1:T(8,128)(4,1)S(1)} %and_and_fusion.2, bf16[512,2,128,1]{0,2,3,1:T(8,128)(2,1)S(1)} %bitcast.72, bf16[256,2,8,128]{3,0,2,1:T(8,128)(2,1)S(1)} %get-tuple-element.448), kind=kOutput, calls=%fused_computation.5.clone.1 | convolution fusion | flops 543158272 | bytes 9846784 | tf_op jit(solution)/shard_map/while/body/eval_jaxpr/rgqd,ngd->gqrn/dot_general | solution.py:44
  356.7 5.3 %fusion.32 = (f32[2,8,256]{2,1,0:T(8,128)}, f32[2,512,256,8]{2,1,3,0:T(8,128)}) fusion(pred[256,512]{0,1:T(8,128)(4,1)S(1)} %and_and_fusion.2, bf16[512,2,128,1]{0,2,3,1:T(8,128)(2,1)S(1)} %bitcast.72, bf16[256,2,8,128]{3,0,2,1:T(8,128)(2,1)S(1)} %get-tuple-element.448), kind=kOutput, calls=%fused_computation.5.clone.1 | convolution fusion | flops 543158272 | bytes 9846784 | tf_op jit(solution)/shard_map/while/body/eval_jaxpr/rgqd,ngd->gqrn/dot_general | solution.py:44
  375.7 5.3 %fusion.32 = (f32[2,8,256]{2,1,0:T(8,128)}, f32[2,512,256,8]{2,1,3,0:T(8,128)}) fusion(pred[256,512]{0,1:T(8,128)(4,1)S(1)} %and_and_fusion.2, bf16[512,2,128,1]{0,2,3,1:T(8,128)(2,1)S(1)} %bitcast.72, bf16[256,2,8,128]{3,0,2,1:T(8,128)(2,1)S(1)} %get-tuple-element.448), kind=kOutput, calls=%fused_computation.5.clone.1 | convolution fusion | flops 543158272 | bytes 9846784 | tf_op jit(solution)/shard_map/while/body/eval_jaxpr/rgqd,ngd->gqrn/dot_general | solution.py:44
  394.8 5.3 %fusion.32 = (f32[2,8,256]{2,1,0:T(8,128)}, f32[2,512,256,8]{2,1,3,0:T(8,128)}) fusion(pred[256,512]{0,1:T(8,128)(4,1)S(1)} %and_and_fusion.2, bf16[512,2,128,1]{0,2,3,1:T(8,128)(2,1)S(1)} %bitcast.72, bf16[256,2,8,128]{3,0,2,1:T(8,128)(2,1)S(1)} %get-tuple-element.448), kind=kOutput, calls=%fused_computation.5.clone.1 | convolution fusion | flops 543158272 | bytes 9846784 | tf_op jit(solution)/shard_map/while/body/eval_jaxpr/rgqd,ngd->gqrn/dot_general | solution.py:44
  413.8 5.3 %fusion.32 = (f32[2,8,256]{2,1,0:T(8,128)}, f32[2,512,256,8]{2,1,3,0:T(8,128)}) fusion(pred[256,512]{0,1:T(8,128)(4,1)S(1)} %and_and_fusion.2, bf16[512,2,128,1]{0,2,3,1:T(8,128)(2,1)S(1)} %bitcast.72, bf16[256,2,8,128]{3,0,2,1:T(8,128)(2,1)S(1)} %get-tuple-element.448), kind=kOutput, calls=%fused_computation.5.clone.1 | convolution fusion | flops 543158272 | bytes 9846784 | tf_op jit(solution)/shard_map/while/body/eval_jaxpr/rgqd,ngd->gqrn/dot_general | solution.py:44
  431.9 22.5 %all_to_all.29 = bf16[32,8,2048]{2,1,0:T(8,128)(2,1)S(1)} all-to-all(bf16[32,8,2048]{2,1,0:T(8,128)(2,1)S(1)} %convert_element_type.56), channel_id=1, replica_groups=mesh['tok'=32,'kv'=4] {'tok'}, dimensions={0} | all-to-all | bytes 2097152 | tf_op jit(solution)/shard_map/all_to_all | solution.py:143
  465.1 14.8 %all-to-all-done.2 = bf16[4,64,2048]{2,1,0:T(8,128)(2,1)S(1)} async-done(((bf16[4,64,2048]{2,1,0:T(8,128)(2,1)}), bf16[4,64,2048]{2,1,0:T(8,128)(2,1)S(1)}, u32[]{:S(2)}, u32[]{:S(2)}) %all-to-all-start.2) | async-done | bytes 1048608 | tf_op jit(solution)/shard_map/all_to_all | solution.py:153
  (329 shorter events, 206.4 us)
Async XLA Ops:
  7.2 9.2 %copy-start.1 = (bf16[256,2048]{1,0:T(8,128)(2,1)S(1)}, bf16[256,2048]{1,0:T(8,128)(2,1)}, u32[]{:S(2)}) copy-start(bf16[256,2048]{1,0:T(8,128)(2,1)} %param.7) | copy-start | bytes 3145732
  7.2 66.6 %all-gather.3.cloned.1.call-start = ((), (), s32[]{:S(2)}) async-start(), calls=%async_computation.3 | async-start | bytes 4325376 | tf_op jit(solution)/shard_map/all_gather | solution.py:137
  14.4 110.2 %all-gather.5.cloned.1.call-start = ((), (), s32[]{:S(2)}) async-start(), calls=%async_computation.4 | async-start | bytes 4325376 | tf_op jit(solution)/shard_map/all_gather | solution.py:138
  22.5 25.9 %all-to-all-start = ((bf16[32,8,2048]{2,1,0:T(8,128)(2,1)}), bf16[32,8,2048]{2,1,0:T(8,128)(2,1)S(1)}, u32[]{:S(2)}, u32[]{:S(2)}) async-start(bf16[32,8,2048]{2,1,0:T(8,128)(2,1)} %broadcast_select_fusion), calls=%async_computation | async-start | bytes 2097152 | tf_op jit(solution)/shard_map/all_to_all | solution.py:119
  134.3 5.9 %copy-start = (f32[2,512,256,8]{2,1,3,0:T(8,128)S(1)}, f32[2,512,256,8]{2,1,3,0:T(8,128)}, u32[]{:S(2)}) copy-start(f32[2,512,256,8]{2,1,3,0:T(8,128)} %get-tuple-element.409) | copy-start | bytes 25165828 | tf_op jit(solution)/shard_map/while
  138.9 4.7 copy-start.3
  153.3 5.9 %copy-start = (f32[2,512,256,8]{2,1,3,0:T(8,128)S(1)}, f32[2,512,256,8]{2,1,3,0:T(8,128)}, u32[]{:S(2)}) copy-start(f32[2,512,256,8]{2,1,3,0:T(8,128)} %get-tuple-element.409) | copy-start | bytes 25165828 | tf_op jit(solution)/shard_map/while
  157.9 4.7 copy-start.3
  172.4 5.9 %copy-start = (f32[2,512,256,8]{2,1,3,0:T(8,128)S(1)}, f32[2,512,256,8]{2,1,3,0:T(8,128)}, u32[]{:S(2)}) copy-start(f32[2,512,256,8]{2,1,3,0:T(8,128)} %get-tuple-element.409) | copy-start | bytes 25165828 | tf_op jit(solution)/shard_map/while
  177.0 4.7 copy-start.3
  191.4 5.9 %copy-start = (f32[2,512,256,8]{2,1,3,0:T(8,128)S(1)}, f32[2,512,256,8]{2,1,3,0:T(8,128)}, u32[]{:S(2)}) copy-start(f32[2,512,256,8]{2,1,3,0:T(8,128)} %get-tuple-element.409) | copy-start | bytes 25165828 | tf_op jit(solution)/shard_map/while
  196.0 4.7 copy-start.3
  210.4 5.9 %copy-start = (f32[2,512,256,8]{2,1,3,0:T(8,128)S(1)}, f32[2,512,256,8]{2,1,3,0:T(8,128)}, u32[]{:S(2)}) copy-start(f32[2,512,256,8]{2,1,3,0:T(8,128)} %get-tuple-element.409) | copy-start | bytes 25165828 | tf_op jit(solution)/shard_map/while
  215.1 4.7 copy-start.3
  229.5 5.9 %copy-start = (f32[2,512,256,8]{2,1,3,0:T(8,128)S(1)}, f32[2,512,256,8]{2,1,3,0:T(8,128)}, u32[]{:S(2)}) copy-start(f32[2,512,256,8]{2,1,3,0:T(8,128)} %get-tuple-element.409) | copy-start | bytes 25165828 | tf_op jit(solution)/shard_map/while
  234.1 4.7 copy-start.3
  248.5 5.9 %copy-start = (f32[2,512,256,8]{2,1,3,0:T(8,128)S(1)}, f32[2,512,256,8]{2,1,3,0:T(8,128)}, u32[]{:S(2)}) copy-start(f32[2,512,256,8]{2,1,3,0:T(8,128)} %get-tuple-element.409) | copy-start | bytes 25165828 | tf_op jit(solution)/shard_map/while
  253.1 4.7 copy-start.3
  267.6 5.9 %copy-start = (f32[2,512,256,8]{2,1,3,0:T(8,128)S(1)}, f32[2,512,256,8]{2,1,3,0:T(8,128)}, u32[]{:S(2)}) copy-start(f32[2,512,256,8]{2,1,3,0:T(8,128)} %get-tuple-element.409) | copy-start | bytes 25165828 | tf_op jit(solution)/shard_map/while
  272.2 4.7 copy-start.3
  286.6 5.9 %copy-start = (f32[2,512,256,8]{2,1,3,0:T(8,128)S(1)}, f32[2,512,256,8]{2,1,3,0:T(8,128)}, u32[]{:S(2)}) copy-start(f32[2,512,256,8]{2,1,3,0:T(8,128)} %get-tuple-element.409) | copy-start | bytes 25165828 | tf_op jit(solution)/shard_map/while
  291.2 4.7 copy-start.3
  305.6 5.9 %copy-start = (f32[2,512,256,8]{2,1,3,0:T(8,128)S(1)}, f32[2,512,256,8]{2,1,3,0:T(8,128)}, u32[]{:S(2)}) copy-start(f32[2,512,256,8]{2,1,3,0:T(8,128)} %get-tuple-element.409) | copy-start | bytes 25165828 | tf_op jit(solution)/shard_map/while
  324.7 5.9 %copy-start = (f32[2,512,256,8]{2,1,3,0:T(8,128)S(1)}, f32[2,512,256,8]{2,1,3,0:T(8,128)}, u32[]{:S(2)}) copy-start(f32[2,512,256,8]{2,1,3,0:T(8,128)} %get-tuple-element.409) | copy-start | bytes 25165828 | tf_op jit(solution)/shard_map/while
  343.7 5.9 %copy-start = (f32[2,512,256,8]{2,1,3,0:T(8,128)S(1)}, f32[2,512,256,8]{2,1,3,0:T(8,128)}, u32[]{:S(2)}) copy-start(f32[2,512,256,8]{2,1,3,0:T(8,128)} %get-tuple-element.409) | copy-start | bytes 25165828 | tf_op jit(solution)/shard_map/while
  362.8 5.9 %copy-start = (f32[2,512,256,8]{2,1,3,0:T(8,128)S(1)}, f32[2,512,256,8]{2,1,3,0:T(8,128)}, u32[]{:S(2)}) copy-start(f32[2,512,256,8]{2,1,3,0:T(8,128)} %get-tuple-element.409) | copy-start | bytes 25165828 | tf_op jit(solution)/shard_map/while
  381.8 5.9 %copy-start = (f32[2,512,256,8]{2,1,3,0:T(8,128)S(1)}, f32[2,512,256,8]{2,1,3,0:T(8,128)}, u32[]{:S(2)}) copy-start(f32[2,512,256,8]{2,1,3,0:T(8,128)} %get-tuple-element.409) | copy-start | bytes 25165828 | tf_op jit(solution)/shard_map/while
  400.8 5.9 %copy-start = (f32[2,512,256,8]{2,1,3,0:T(8,128)S(1)}, f32[2,512,256,8]{2,1,3,0:T(8,128)}, u32[]{:S(2)}) copy-start(f32[2,512,256,8]{2,1,3,0:T(8,128)} %get-tuple-element.409) | copy-start | bytes 25165828 | tf_op jit(solution)/shard_map/while
  419.9 5.9 %copy-start = (f32[2,512,256,8]{2,1,3,0:T(8,128)S(1)}, f32[2,512,256,8]{2,1,3,0:T(8,128)}, u32[]{:S(2)}) copy-start(f32[2,512,256,8]{2,1,3,0:T(8,128)} %get-tuple-element.409) | copy-start | bytes 25165828 | tf_op jit(solution)/shard_map/while
  431.9 23.6 %copy-start.6 = (s32[32]{0:T(128)S(1)}, s32[32]{0:T(128)}, u32[]{:S(2)}) copy-start(s32[32]{0:T(128)} %copy-done.5) | copy-start | bytes 388
  455.5 9.0 %copy-start.4 = (f32[2,8,256]{2,1,0:T(8,128)S(1)}, f32[2,8,256]{2,1,0:T(8,128)}, u32[]{:S(2)}) copy-start(f32[2,8,256]{2,1,0:T(8,128)} %get-tuple-element.238) | copy-start | bytes 49156
  460.1 19.8 %all-to-all-start.2 = ((bf16[4,64,2048]{2,1,0:T(8,128)(2,1)}), bf16[4,64,2048]{2,1,0:T(8,128)(2,1)S(1)}, u32[]{:S(2)}, u32[]{:S(2)}) async-start(bf16[4,64,2048]{2,1,0:T(8,128)(2,1)} %bitcast.7), calls=%async_computation.2 | async-start | bytes 2097152 | tf_op jit(solution)/shard_map/all_to_all | solution.py:153
  (24 other events, 107.2 us)
Sparse Core Ops, SparseCore 0:
  14.5 59.1 all-gather.2
  75.9 48.6 all-gather.4
where the time goes:
time: 490 us; the launch traced here: 488 us
  matrix products  141 us (29%)
  other arithmetic  136 us (28%)
  waiting for transfers between devices  109 us (22%)
  local copies, waits for them, and re-layouts  51.6 us (11%)
  blocking collectives  22.5 us (5%)
  between operations  14.2 us (3%)
  starting transfers between devices  12.1 us (2%)
    dot_general x16, matrix products, attend_block(): jnp.einsum('rgqd,ngd->gqrn', query_rows, key_rows, preferred_element_type...  85.4 us
    reduce_sum x16, other arithmetic, attend_block(): row_sum = row_sum * factor + jnp.sum(weights, axis=-1)  73.4 us
    dot_general x16, matrix products, attend_block(): jnp.einsum('gqrn,ngd->gqrd', probs, value_rows, preferred_element_type=jn...  55.7 us
    all_gather x1, waiting for transfers between devices, body(): lax.all_gather(value_states, 'tok', axis=0, tiled=True)  50.9 us
    all_gather x1, waiting for transfers between devices, body(): lax.all_gather(k_rot, 'tok', axis=0, tiled=True)  24.8 us
    all_to_all x1, blocking collectives, body(): lax.all_to_all(result.reshape(shards, block_rows, q_local * HEAD_DIM), 't...  22.5 us
    while x112, local copies, waits for them, and re-layouts  19.7 us
    all_to_all x1, waiting for transfers between devices, body(): lax.all_to_all(outgoing, 'tok', split_axis=0, concat_axis=0, tiled=True)  18.3 us
  transfers between devices with their start and end apart: 4, of which 4 were waited for; matrix products, arithmetic and copies ran while one was open for 2% of the time, Pallas kernels for 0%

commit v1 on v0

--- a/solution.py
+++ b/solution.py
@@ -1,13 +1,27 @@
+import functools
 from functools import partial
 import math
 import jax
 import jax.numpy as jnp
 from jax import lax
 from jax.sharding import PartitionSpec as P
+from jax.lax import all_to_all, axis_size
 
 HEAD_DIM = 128
 THETA = 500000.0
 NEG = -1e30
+
+
+def create_goods(matrix, bus_axis):
+    return jnp.concatenate(
+        all_to_all(
+            jnp.stack(tuple((matrix for _ in range(axis_size(bus_axis)))), axis=0), bus_axis, 0, 0
+        ),
+        0,
+    )
+
+
+samples_prepare = functools.partial(create_goods, bus_axis="tok")
 
 
 def doc_layout(doc_lengths, token_index):
@@ -133,10 +147,7 @@
     )
     final_state = folder(
         initial,
-        (
-            lax.all_gather(k_rot, "tok", axis=0, tiled=True),
-            lax.all_gather(value_states, "tok", axis=0, tiled=True),
-        ),
+        (samples_prepare(k_rot), lax.all_gather(value_states, "tok", axis=0, tiled=True)),
         jnp.int32(0),
     )
     result, served_lse = finish(final_state, tok_dev, q_local)

time: 490 us -> 507 us (1.035)
  local copies, waits for them, and re-layouts: 51.6 us -> 81.1 us
  waiting for transfers between devices: 109 us -> 87.6 us
  starting transfers between devices: 12.1 us -> 18.2 us
    all_to_all x0 -> x1, waiting for transfers between devices: none -> 56.7 us  [create_goods(): all_to_all(jnp.stack(tuple((matrix for _ in range(axis_size(bus_axis)))),...]
    all_gather x1, waiting for transfers between devices: 50.9 us -> 0.01 us  [body(): lax.all_gather(value_states, 'tok', axis=0, tiled=True)]
    all_gather x1 -> x0, waiting for transfers between devices: 24.8 us -> none  [body(): lax.all_gather(k_rot, 'tok', axis=0, tiled=True)]
    dynamic_slice x0 -> x32, local copies, waits for them, and re-layouts: none -> 17.8 us  [inner(): lax.dynamic_slice_in_dim(key_piece, offset, stride, 0)]
    all_to_all x0 -> x1, local copies, waits for them, and re-layouts: none -> 6.49 us  [create_goods(): all_to_all(jnp.stack(tuple((matrix for _ in range(axis_size(bus_axis)))),...]
    while x112 -> x176, local copies, waits for them, and re-layouts: 19.7 us -> 21.4 us
  transfers between devices with their start and end apart: 4 -> 4, of which waited for: 4 -> 3; matrix products, arithmetic and copies ran while one was open for 2% -> 5% of each run, Pallas kernels for 0% -> 0%
where the time goes in v1:
time: 507 us; the launch traced here: 505 us
  matrix products  143 us (28%)
  other arithmetic  138 us (27%)
  waiting for transfers between devices  87.6 us (17%)
  local copies, waits for them, and re-layouts  81.1 us (16%)
  blocking collectives  21.1 us (4%)
  starting transfers between devices  18.2 us (4%)
  between operations  14.2 us (3%)
    dot_general x16, matrix products, attend_block(): jnp.einsum('rgqd,ngd->gqrn', query_rows, key_rows, preferred_element_type...  87.2 us
    reduce_sum x16, other arithmetic, attend_block(): row_sum = row_sum * factor + jnp.sum(weights, axis=-1)  73.4 us
    all_to_all x1, waiting for transfers between devices, create_goods(): all_to_all(jnp.stack(tuple((matrix for _ in range(axis_size(bus_axis)))),...  56.7 us
    dot_general x16, matrix products, attend_block(): jnp.einsum('gqrn,ngd->gqrd', probs, value_rows, preferred_element_type=jn...  55.7 us
    while x176, local copies, waits for them, and re-layouts  21.4 us
    all_to_all x1, blocking collectives, body(): lax.all_to_all(result.reshape(shards, block_rows, q_local * HEAD_DIM), 't...  21.1 us
    dynamic_slice x16, local copies, waits for them, and re-layouts, inner(): lax.dynamic_slice_in_dim(value_piece, offset, stride, 0)  19 us
    dynamic_slice x32, local copies, waits for them, and re-layouts, inner(): lax.dynamic_slice_in_dim(key_piece, offset, stride, 0)  17.8 us
  transfers between devices with their start and end apart: 4, of which 3 were waited for; matrix products, arithmetic and copies ran while one was open for 5% of the time, Pallas kernels for 0%

profile of v1, /device:TPU:0, one launch (start us, length us, event | category | flops | bytes accessed | tf_op | source)
XLA Modules:
  0.0 504.6 jit_solution(4118121220097687441)
XLA Ops:
  21.9 7.4 %all-to-all-start.1 = ((bf16[32,8,2048]{2,1,0:T(8,128)(2,1)}), bf16[32,8,2048]{2,1,0:T(8,128)(2,1)S(1)}, u32[]{:S(2)}, u32[]{:S(2)}) async-start(bf16[32,8,2048]{2,1,0:T(8,128)(2,1)} %broadcast_select_fusion), calls=%async_computation.1 | async-start | bytes 2097152 | tf_op jit(solution)/shard_map/all_to_all | solution.py:133
  30.4 16.2 %all-to-all-done.1 = bf16[32,8,2048]{2,1,0:T(8,128)(2,1)S(1)} async-done(((bf16[32,8,2048]{2,1,0:T(8,128)(2,1)}), bf16[32,8,2048]{2,1,0:T(8,128)(2,1)S(1)}, u32[]{:S(2)}, u32[]{:S(2)}) %all-to-all-start.1) | async-done | bytes 1048608 | tf_op jit(solution)/shard_map/all_to_all | solution.py:133
  49.1 5.1 %all-to-all-start = ((bf16[32,256,256]{1,2,0:T(8,128)(2,1)}), bf16[32,256,256]{1,2,0:T(8,128)(2,1)}, u32[]{:S(2)}, u32[]{:S(2)}) async-start(bf16[32,256,256]{1,2,0:T(8,128)(2,1)} %stack.2), calls=%async_computation | async-start | bytes 8388608 | tf_op jit(solution)/shard_map/all_to_all | solution.py:17
  54.7 56.7 %all-to-all-done = bf16[32,256,256]{1,2,0:T(8,128)(2,1)} async-done(((bf16[32,256,256]{1,2,0:T(8,128)(2,1)}), bf16[32,256,256]{1,2,0:T(8,128)(2,1)}, u32[]{:S(2)}, u32[]{:S(2)}) %all-to-all-start) | async-done | bytes 4194336 | tf_op jit(solution)/shard_map/all_to_all | solution.py:17
  111.4 6.5 %copy.45 = bf16[32,256,256]{2,1,0:T(8,128)(2,1)} copy(bf16[32,256,256]{1,2,0:T(8,128)(2,1)} %all-to-all-done) | data formatting | bytes 8388608 | tf_op jit(solution)/shard_map/all_to_all | solution.py:17
  117.9 327.8 %while.20 = (s32[]{:T(128)}, f32[2,8,256]{2,1,0:T(8,128)S(1)}, f32[2,8,256]{2,1,0:T(8,128)}, f32[2,8,256,128]{3,2,1,0:T(8,128)}, s32[256]{0:T(256)}, /*index=5*/...) while((s32[]{:T(128)}, f32[2,8,256]{2,1,0:T(8,128)S(1)}, ...), condition=%wide.region_7.8_spmd.clone, body=%wide.region_3.7_spmd.clone.sunk | while | flops 1103148288 | bytes 83771936 | solution.py:100
  121.5 5.4 %fusion.32 = (f32[2,8,256]{2,1,0:T(8,128)}, f32[2,512,256,8]{2,1,3,0:T(8,128)}) fusion(pred[256,512]{0,1:T(8,128)(4,1)S(1)} %and_and_fusion.2, bf16[512,2,128,1]{0,2,3,1:T(8,128)(2,1)S(1)} %bitcast.72, bf16[256,2,8,128]{3,0,2,1:T(8,128)(2,1)S(1)} %get-tuple-element.462), kind=kOutput, calls=%fused_computation.5.clone.1 | convolution fusion | flops 543158272 | bytes 9846784 | tf_op jit(solution)/shard_map/while/body/eval_jaxpr/rgqd,ngd->gqrn/dot_general | solution.py:58
  127.7 4.6 fusion.33
  142.0 5.4 %fusion.32 = (f32[2,8,256]{2,1,0:T(8,128)}, f32[2,512,256,8]{2,1,3,0:T(8,128)}) fusion(pred[256,512]{0,1:T(8,128)(4,1)S(1)} %and_and_fusion.2, bf16[512,2,128,1]{0,2,3,1:T(8,128)(2,1)S(1)} %bitcast.72, bf16[256,2,8,128]{3,0,2,1:T(8,128)(2,1)S(1)} %get-tuple-element.462), kind=kOutput, calls=%fused_computation.5.clone.1 | convolution fusion | flops 543158272 | bytes 9846784 | tf_op jit(solution)/shard_map/while/body/eval_jaxpr/rgqd,ngd->gqrn/dot_general | solution.py:58
  148.2 4.6 fusion.33
  162.5 5.4 %fusion.32 = (f32[2,8,256]{2,1,0:T(8,128)}, f32[2,512,256,8]{2,1,3,0:T(8,128)}) fusion(pred[256,512]{0,1:T(8,128)(4,1)S(1)} %and_and_fusion.2, bf16[512,2,128,1]{0,2,3,1:T(8,128)(2,1)S(1)} %bitcast.72, bf16[256,2,8,128]{3,0,2,1:T(8,128)(2,1)S(1)} %get-tuple-element.462), kind=kOutput, calls=%fused_computation.5.clone.1 | convolution fusion | flops 543158272 | bytes 9846784 | tf_op jit(solution)/shard_map/while/body/eval_jaxpr/rgqd,ngd->gqrn/dot_general | solution.py:58
  168.7 4.6 fusion.33
  183.0 5.4 %fusion.32 = (f32[2,8,256]{2,1,0:T(8,128)}, f32[2,512,256,8]{2,1,3,0:T(8,128)}) fusion(pred[256,512]{0,1:T(8,128)(4,1)S(1)} %and_and_fusion.2, bf16[512,2,128,1]{0,2,3,1:T(8,128)(2,1)S(1)} %bitcast.72, bf16[256,2,8,128]{3,0,2,1:T(8,128)(2,1)S(1)} %get-tuple-element.462), kind=kOutput, calls=%fused_computation.5.clone.1 | convolution fusion | flops 543158272 | bytes 9846784 | tf_op jit(solution)/shard_map/while/body/eval_jaxpr/rgqd,ngd->gqrn/dot_general | solution.py:58
  189.2 4.6 fusion.33
  203.5 5.4 %fusion.32 = (f32[2,8,256]{2,1,0:T(8,128)}, f32[2,512,256,8]{2,1,3,0:T(8,128)}) fusion(pred[256,512]{0,1:T(8,128)(4,1)S(1)} %and_and_fusion.2, bf16[512,2,128,1]{0,2,3,1:T(8,128)(2,1)S(1)} %bitcast.72, bf16[256,2,8,128]{3,0,2,1:T(8,128)(2,1)S(1)} %get-tuple-element.462), kind=kOutput, calls=%fused_computation.5.clone.1 | convolution fusion | flops 543158272 | bytes 9846784 | tf_op jit(solution)/shard_map/while/body/eval_jaxpr/rgqd,ngd->gqrn/dot_general | solution.py:58
  209.7 4.6 fusion.33
  224.0 5.4 %fusion.32 = (f32[2,8,256]{2,1,0:T(8,128)}, f32[2,512,256,8]{2,1,3,0:T(8,128)}) fusion(pred[256,512]{0,1:T(8,128)(4,1)S(1)} %and_and_fusion.2, bf16[512,2,128,1]{0,2,3,1:T(8,128)(2,1)S(1)} %bitcast.72, bf16[256,2,8,128]{3,0,2,1:T(8,128)(2,1)S(1)} %get-tuple-element.462), kind=kOutput, calls=%fused_computation.5.clone.1 | convolution fusion | flops 543158272 | bytes 9846784 | tf_op jit(solution)/shard_map/while/body/eval_jaxpr/rgqd,ngd->gqrn/dot_general | solution.py:58
  230.1 4.6 fusion.33
  244.5 5.4 %fusion.32 = (f32[2,8,256]{2,1,0:T(8,128)}, f32[2,512,256,8]{2,1,3,0:T(8,128)}) fusion(pred[256,512]{0,1:T(8,128)(4,1)S(1)} %and_and_fusion.2, bf16[512,2,128,1]{0,2,3,1:T(8,128)(2,1)S(1)} %bitcast.72, bf16[256,2,8,128]{3,0,2,1:T(8,128)(2,1)S(1)} %get-tuple-element.462), kind=kOutput, calls=%fused_computation.5.clone.1 | convolution fusion | flops 543158272 | bytes 9846784 | tf_op jit(solution)/shard_map/while/body/eval_jaxpr/rgqd,ngd->gqrn/dot_general | solution.py:58
  250.6 4.6 fusion.33
  265.0 5.4 %fusion.32 = (f32[2,8,256]{2,1,0:T(8,128)}, f32[2,512,256,8]{2,1,3,0:T(8,128)}) fusion(pred[256,512]{0,1:T(8,128)(4,1)S(1)} %and_and_fusion.2, bf16[512,2,128,1]{0,2,3,1:T(8,128)(2,1)S(1)} %bitcast.72, bf16[256,2,8,128]{3,0,2,1:T(8,128)(2,1)S(1)} %get-tuple-element.462), kind=kOutput, calls=%fused_computation.5.clone.1 | convolution fusion | flops 543158272 | bytes 9846784 | tf_op jit(solution)/shard_map/while/body/eval_jaxpr/rgqd,ngd->gqrn/dot_general | solution.py:58
  285.4 5.4 %fusion.32 = (f32[2,8,256]{2,1,0:T(8,128)}, f32[2,512,256,8]{2,1,3,0:T(8,128)}) fusion(pred[256,512]{0,1:T(8,128)(4,1)S(1)} %and_and_fusion.2, bf16[512,2,128,1]{0,2,3,1:T(8,128)(2,1)S(1)} %bitcast.72, bf16[256,2,8,128]{3,0,2,1:T(8,128)(2,1)S(1)} %get-tuple-element.462), kind=kOutput, calls=%fused_computation.5.clone.1 | convolution fusion | flops 543158272 | bytes 9846784 | tf_op jit(solution)/shard_map/while/body/eval_jaxpr/rgqd,ngd->gqrn/dot_general | solution.py:58
  305.9 5.4 %fusion.32 = (f32[2,8,256]{2,1,0:T(8,128)}, f32[2,512,256,8]{2,1,3,0:T(8,128)}) fusion(pred[256,512]{0,1:T(8,128)(4,1)S(1)} %and_and_fusion.2, bf16[512,2,128,1]{0,2,3,1:T(8,128)(2,1)S(1)} %bitcast.72, bf16[256,2,8,128]{3,0,2,1:T(8,128)(2,1)S(1)} %get-tuple-element.462), kind=kOutput, calls=%fused_computation.5.clone.1 | convolution fusion | flops 543158272 | bytes 9846784 | tf_op jit(solution)/shard_map/while/body/eval_jaxpr/rgqd,ngd->gqrn/dot_general | solution.py:58
  326.4 5.4 %fusion.32 = (f32[2,8,256]{2,1,0:T(8,128)}, f32[2,512,256,8]{2,1,3,0:T(8,128)}) fusion(pred[256,512]{0,1:T(8,128)(4,1)S(1)} %and_and_fusion.2, bf16[512,2,128,1]{0,2,3,1:T(8,128)(2,1)S(1)} %bitcast.72, bf16[256,2,8,128]{3,0,2,1:T(8,128)(2,1)S(1)} %get-tuple-element.462), kind=kOutput, calls=%fused_computation.5.clone.1 | convolution fusion | flops 543158272 | bytes 9846784 | tf_op jit(solution)/shard_map/while/body/eval_jaxpr/rgqd,ngd->gqrn/dot_general | solution.py:58
  346.9 5.4 %fusion.32 = (f32[2,8,256]{2,1,0:T(8,128)}, f32[2,512,256,8]{2,1,3,0:T(8,128)}) fusion(pred[256,512]{0,1:T(8,128)(4,1)S(1)} %and_and_fusion.2, bf16[512,2,128,1]{0,2,3,1:T(8,128)(2,1)S(1)} %bitcast.72, bf16[256,2,8,128]{3,0,2,1:T(8,128)(2,1)S(1)} %get-tuple-element.462), kind=kOutput, calls=%fused_computation.5.clone.1 | convolution fusion | flops 543158272 | bytes 9846784 | tf_op jit(solution)/shard_map/while/body/eval_jaxpr/rgqd,ngd->gqrn/dot_general | solution.py:58
  367.4 5.4 %fusion.32 = (f32[2,8,256]{2,1,0:T(8,128)}, f32[2,512,256,8]{2,1,3,0:T(8,128)}) fusion(pred[256,512]{0,1:T(8,128)(4,1)S(1)} %and_and_fusion.2, bf16[512,2,128,1]{0,2,3,1:T(8,128)(2,1)S(1)} %bitcast.72, bf16[256,2,8,128]{3,0,2,1:T(8,128)(2,1)S(1)} %get-tuple-element.462), kind=kOutput, calls=%fused_computation.5.clone.1 | convolution fusion | flops 543158272 | bytes 9846784 | tf_op jit(solution)/shard_map/while/body/eval_jaxpr/rgqd,ngd->gqrn/dot_general | solution.py:58
  387.9 5.4 %fusion.32 = (f32[2,8,256]{2,1,0:T(8,128)}, f32[2,512,256,8]{2,1,3,0:T(8,128)}) fusion(pred[256,512]{0,1:T(8,128)(4,1)S(1)} %and_and_fusion.2, bf16[512,2,128,1]{0,2,3,1:T(8,128)(2,1)S(1)} %bitcast.72, bf16[256,2,8,128]{3,0,2,1:T(8,128)(2,1)S(1)} %get-tuple-element.462), kind=kOutput, calls=%fused_computation.5.clone.1 | convolution fusion | flops 543158272 | bytes 9846784 | tf_op jit(solution)/shard_map/while/body/eval_jaxpr/rgqd,ngd->gqrn/dot_general | solution.py:58
  408.4 5.4 %fusion.32 = (f32[2,8,256]{2,1,0:T(8,128)}, f32[2,512,256,8]{2,1,3,0:T(8,128)}) fusion(pred[256,512]{0,1:T(8,128)(4,1)S(1)} %and_and_fusion.2, bf16[512,2,128,1]{0,2,3,1:T(8,128)(2,1)S(1)} %bitcast.72, bf16[256,2,8,128]{3,0,2,1:T(8,128)(2,1)S(1)} %get-tuple-element.462), kind=kOutput, calls=%fused_computation.5.clone.1 | convolution fusion | flops 543158272 | bytes 9846784 | tf_op jit(solution)/shard_map/while/body/eval_jaxpr/rgqd,ngd->gqrn/dot_general | solution.py:58
  428.9 5.4 %fusion.32 = (f32[2,8,256]{2,1,0:T(8,128)}, f32[2,512,256,8]{2,1,3,0:T(8,128)}) fusion(pred[256,512]{0,1:T(8,128)(4,1)S(1)} %and_and_fusion.2, bf16[512,2,128,1]{0,2,3,1:T(8,128)(2,1)S(1)} %bitcast.72, bf16[256,2,8,128]{3,0,2,1:T(8,128)(2,1)S(1)} %get-tuple-element.462), kind=kOutput, calls=%fused_computation.5.clone.1 | convolution fusion | flops 543158272 | bytes 9846784 | tf_op jit(solution)/shard_map/while/body/eval_jaxpr/rgqd,ngd->gqrn/dot_general | solution.py:58
  448.9 21.1 %all_to_all.34 = bf16[32,8,2048]{2,1,0:T(8,128)(2,1)S(1)} all-to-all(bf16[32,8,2048]{2,1,0:T(8,128)(2,1)S(1)} %convert_element_type.58), channel_id=1, replica_groups=mesh['tok'=32,'kv'=4] {'tok'}, dimensions={0} | all-to-all | bytes 2097152 | tf_op jit(solution)/shard_map/all_to_all | solution.py:154
  475.7 5.7 %all-to-all-start.3 = ((bf16[4,64,2048]{2,1,0:T(8,128)(2,1)}), bf16[4,64,2048]{2,1,0:T(8,128)(2,1)S(1)}, u32[]{:S(2)}, u32[]{:S(2)}) async-start(bf16[4,64,2048]{2,1,0:T(8,128)(2,1)} %bitcast.8), calls=%async_computation.3 | async-start | bytes 2097152 | tf_op jit(solution)/shard_map/all_to_all | solution.py:164
  482.0 14.8 %all-to-all-done.3 = bf16[4,64,2048]{2,1,0:T(8,128)(2,1)S(1)} async-done(((bf16[4,64,2048]{2,1,0:T(8,128)(2,1)}), bf16[4,64,2048]{2,1,0:T(8,128)(2,1)S(1)}, u32[]{:S(2)}, u32[]{:S(2)}) %all-to-all-start.3) | async-done | bytes 1048608 | tf_op jit(solution)/shard_map/all_to_all | solution.py:164
  (427 shorter events, 235.9 us)
Async XLA Ops:
  7.2 7.3 %copy-start.9 = (s32[16]{0:T(128)S(1)}, s32[16]{0:T(128)}, u32[]{:S(2)}) copy-start(s32[16]{0:T(128)} %param.10) | copy-start | bytes 196
  7.2 110.7 %all-gather.2.cloned.1.call-start = ((), (), s32[]{:S(2)}) async-start(), calls=%async_computation.4 | async-start | bytes 4325376 | tf_op jit(solution)/shard_map/all_gather | solution.py:150
  17.7 11.6 %copy-start.6 = (bf16[256,256]{1,0:T(8,128)(2,1)S(1)}, bf16[256,256]{1,0:T(8,128)(2,1)}, u32[]{:S(2)}) copy-start(bf16[256,256]{1,0:T(8,128)(2,1)} %param.8) | copy-start | bytes 393220
  21.9 24.7 %all-to-all-start.1 = ((bf16[32,8,2048]{2,1,0:T(8,128)(2,1)}), bf16[32,8,2048]{2,1,0:T(8,128)(2,1)S(1)}, u32[]{:S(2)}, u32[]{:S(2)}) async-start(bf16[32,8,2048]{2,1,0:T(8,128)(2,1)} %broadcast_select_fusion), calls=%async_computation.1 | async-start | bytes 2097152 | tf_op jit(solution)/shard_map/all_to_all | solution.py:133
  49.1 62.3 %all-to-all-start = ((bf16[32,256,256]{1,2,0:T(8,128)(2,1)}), bf16[32,256,256]{1,2,0:T(8,128)(2,1)}, u32[]{:S(2)}, u32[]{:S(2)}) async-start(bf16[32,256,256]{1,2,0:T(8,128)(2,1)} %stack.2), calls=%async_computation | async-start | bytes 8388608 | tf_op jit(solution)/shard_map/all_to_all | solution.py:17
  121.5 12.0 %copy-start.1 = (f32[2,8,256,128]{3,2,1,0:T(8,128)S(1)}, f32[2,8,256,128]{3,2,1,0:T(8,128)}, u32[]{:S(2)}) copy-start(f32[2,8,256,128]{3,2,1,0:T(8,128)} %get-tuple-element.444) | copy-start | bytes 6291460 | tf_op jit(solution)/shard_map/while
  127.7 5.9 %copy-start = (f32[2,512,256,8]{2,1,3,0:T(8,128)S(1)}, f32[2,512,256,8]{2,1,3,0:T(8,128)}, u32[]{:S(2)}) copy-start(f32[2,512,256,8]{2,1,3,0:T(8,128)} %get-tuple-element.424) | copy-start | bytes 25165828 | tf_op jit(solution)/shard_map/while
  142.0 12.0 %copy-start.1 = (f32[2,8,256,128]{3,2,1,0:T(8,128)S(1)}, f32[2,8,256,128]{3,2,1,0:T(8,128)}, u32[]{:S(2)}) copy-start(f32[2,8,256,128]{3,2,1,0:T(8,128)} %get-tuple-element.444) | copy-start | bytes 6291460 | tf_op jit(solution)/shard_map/while
  148.2 5.9 %copy-start = (f32[2,512,256,8]{2,1,3,0:T(8,128)S(1)}, f32[2,512,256,8]{2,1,3,0:T(8,128)}, u32[]{:S(2)}) copy-start(f32[2,512,256,8]{2,1,3,0:T(8,128)} %get-tuple-element.424) | copy-start | bytes 25165828 | tf_op jit(solution)/shard_map/while
  162.5 12.0 %copy-start.1 = (f32[2,8,256,128]{3,2,1,0:T(8,128)S(1)}, f32[2,8,256,128]{3,2,1,0:T(8,128)}, u32[]{:S(2)}) copy-start(f32[2,8,256,128]{3,2,1,0:T(8,128)} %get-tuple-element.444) | copy-start | bytes 6291460 | tf_op jit(solution)/shard_map/while
  168.7 5.9 %copy-start = (f32[2,512,256,8]{2,1,3,0:T(8,128)S(1)}, f32[2,512,256,8]{2,1,3,0:T(8,128)}, u32[]{:S(2)}) copy-start(f32[2,512,256,8]{2,1,3,0:T(8,128)} %get-tuple-element.424) | copy-start | bytes 25165828 | tf_op jit(solution)/shard_map/while
  183.0 12.0 %copy-start.1 = (f32[2,8,256,128]{3,2,1,0:T(8,128)S(1)}, f32[2,8,256,128]{3,2,1,0:T(8,128)}, u32[]{:S(2)}) copy-start(f32[2,8,256,128]{3,2,1,0:T(8,128)} %get-tuple-element.444) | copy-start | bytes 6291460 | tf_op jit(solution)/shard_map/while
  189.2 5.9 %copy-start = (f32[2,512,256,8]{2,1,3,0:T(8,128)S(1)}, f32[2,512,256,8]{2,1,3,0:T(8,128)}, u32[]{:S(2)}) copy-start(f32[2,512,256,8]{2,1,3,0:T(8,128)} %get-tuple-element.424) | copy-start | bytes 25165828 | tf_op jit(solution)/shard_map/while
  203.5 12.0 %copy-start.1 = (f32[2,8,256,128]{3,2,1,0:T(8,128)S(1)}, f32[2,8,256,128]{3,2,1,0:T(8,128)}, u32[]{:S(2)}) copy-start(f32[2,8,256,128]{3,2,1,0:T(8,128)} %get-tuple-element.444) | copy-start | bytes 6291460 | tf_op jit(solution)/shard_map/while
  209.7 5.9 %copy-start = (f32[2,512,256,8]{2,1,3,0:T(8,128)S(1)}, f32[2,512,256,8]{2,1,3,0:T(8,128)}, u32[]{:S(2)}) copy-start(f32[2,512,256,8]{2,1,3,0:T(8,128)} %get-tuple-element.424) | copy-start | bytes 25165828 | tf_op jit(solution)/shard_map/while
  224.0 12.0 %copy-start.1 = (f32[2,8,256,128]{3,2,1,0:T(8,128)S(1)}, f32[2,8,256,128]{3,2,1,0:T(8,128)}, u32[]{:S(2)}) copy-start(f32[2,8,256,128]{3,2,1,0:T(8,128)} %get-tuple-element.444) | copy-start | bytes 6291460 | tf_op jit(solution)/shard_map/while
  230.1 5.9 %copy-start = (f32[2,512,256,8]{2,1,3,0:T(8,128)S(1)}, f32[2,512,256,8]{2,1,3,0:T(8,128)}, u32[]{:S(2)}) copy-start(f32[2,512,256,8]{2,1,3,0:T(8,128)} %get-tuple-element.424) | copy-start | bytes 25165828 | tf_op jit(solution)/shard_map/while
  244.5 12.0 %copy-start.1 = (f32[2,8,256,128]{3,2,1,0:T(8,128)S(1)}, f32[2,8,256,128]{3,2,1,0:T(8,128)}, u32[]{:S(2)}) copy-start(f32[2,8,256,128]{3,2,1,0:T(8,128)} %get-tuple-element.444) | copy-start | bytes 6291460 | tf_op jit(solution)/shard_map/while
  264.9 12.0 %copy-start.1 = (f32[2,8,256,128]{3,2,1,0:T(8,128)S(1)}, f32[2,8,256,128]{3,2,1,0:T(8,128)}, u32[]{:S(2)}) copy-start(f32[2,8,256,128]{3,2,1,0:T(8,128)} %get-tuple-element.444) | copy-start | bytes 6291460 | tf_op jit(solution)/shard_map/while
  271.1 5.9 %copy-start = (f32[2,512,256,8]{2,1,3,0:T(8,128)S(1)}, f32[2,512,256,8]{2,1,3,0:T(8,128)}, u32[]{:S(2)}) copy-start(f32[2,512,256,8]{2,1,3,0:T(8,128)} %get-tuple-element.424) | copy-start | bytes 25165828 | tf_op jit(solution)/shard_map/while
  285.4 12.0 %copy-start.1 = (f32[2,8,256,128]{3,2,1,0:T(8,128)S(1)}, f32[2,8,256,128]{3,2,1,0:T(8,128)}, u32[]{:S(2)}) copy-start(f32[2,8,256,128]{3,2,1,0:T(8,128)} %get-tuple-element.444) | copy-start | bytes 6291460 | tf_op jit(solution)/shard_map/while
  305.9 12.0 %copy-start.1 = (f32[2,8,256,128]{3,2,1,0:T(8,128)S(1)}, f32[2,8,256,128]{3,2,1,0:T(8,128)}, u32[]{:S(2)}) copy-start(f32[2,8,256,128]{3,2,1,0:T(8,128)} %get-tuple-element.444) | copy-start | bytes 6291460 | tf_op jit(solution)/shard_map/while
  326.4 12.0 %copy-start.1 = (f32[2,8,256,128]{3,2,1,0:T(8,128)S(1)}, f32[2,8,256,128]{3,2,1,0:T(8,128)}, u32[]{:S(2)}) copy-start(f32[2,8,256,128]{3,2,1,0:T(8,128)} %get-tuple-element.444) | copy-start | bytes 6291460 | tf_op jit(solution)/shard_map/while
  346.9 12.0 %copy-start.1 = (f32[2,8,256,128]{3,2,1,0:T(8,128)S(1)}, f32[2,8,256,128]{3,2,1,0:T(8,128)}, u32[]{:S(2)}) copy-start(f32[2,8,256,128]{3,2,1,0:T(8,128)} %get-tuple-element.444) | copy-start | bytes 6291460 | tf_op jit(solution)/shard_map/while
  353.1 5.9 %copy-start = (f32[2,512,256,8]{2,1,3,0:T(8,128)S(1)}, f32[2,512,256,8]{2,1,3,0:T(8,128)}, u32[]{:S(2)}) copy-start(f32[2,512,256,8]{2,1,3,0:T(8,128)} %get-tuple-element.424) | copy-start | bytes 25165828 | tf_op jit(solution)/shard_map/while
  367.4 12.0 %copy-start.1 = (f32[2,8,256,128]{3,2,1,0:T(8,128)S(1)}, f32[2,8,256,128]{3,2,1,0:T(8,128)}, u32[]{:S(2)}) copy-start(f32[2,8,256,128]{3,2,1,0:T(8,128)} %get-tuple-element.444) | copy-start | bytes 6291460 | tf_op jit(solution)/shard_map/while
  387.9 12.0 %copy-start.1 = (f32[2,8,256,128]{3,2,1,0:T(8,128)S(1)}, f32[2,8,256,128]{3,2,1,0:T(8,128)}, u32[]{:S(2)}) copy-start(f32[2,8,256,128]{3,2,1,0:T(8,128)} %get-tuple-element.444) | copy-start | bytes 6291460 | tf_op jit(solution)/shard_map/while
  408.4 12.0 %copy-start.1 = (f32[2,8,256,128]{3,2,1,0:T(8,128)S(1)}, f32[2,8,256,128]{3,2,1,0:T(8,128)}, u32[]{:S(2)}) copy-start(f32[2,8,256,128]{3,2,1,0:T(8,128)} %get-tuple-element.444) | copy-start | bytes 6291460 | tf_op jit(solution)/shard_map/while
  428.9 12.0 %copy-start.1 = (f32[2,8,256,128]{3,2,1,0:T(8,128)S(1)}, f32[2,8,256,128]{3,2,1,0:T(8,128)}, u32[]{:S(2)}) copy-start(f32[2,8,256,128]{3,2,1,0:T(8,128)} %get-tuple-element.444) | copy-start | bytes 6291460 | tf_op jit(solution)/shard_map/while
  447.7 23.4 %copy-start.8 = (s32[32]{0:T(128)S(1)}, s32[32]{0:T(128)}, u32[]{:S(2)}) copy-start(s32[32]{0:T(128)} %copy-done.7) | copy-start | bytes 388
  448.9 32.5 %copy-start.5 = (f32[2,8,256]{2,1,0:T(8,128)S(1)}, f32[2,8,256]{2,1,0:T(8,128)}, u32[]{:S(2)}) copy-start(f32[2,8,256]{2,1,0:T(8,128)} %get-tuple-element.238) | copy-start | bytes 49156
  475.7 21.1 %all-to-all-start.3 = ((bf16[4,64,2048]{2,1,0:T(8,128)(2,1)}), bf16[4,64,2048]{2,1,0:T(8,128)(2,1)S(1)}, u32[]{:S(2)}, u32[]{:S(2)}) async-start(bf16[4,64,2048]{2,1,0:T(8,128)(2,1)} %bitcast.8), calls=%async_computation.3 | async-start | bytes 2097152 | tf_op jit(solution)/shard_map/all_to_all | solution.py:164
  (57 other events, 217.7 us)
Sparse Core Ops, SparseCore 0:
  10.2 84.6 all-gather.1
